TPU v7x, 32 devices: a whole 2x2x4 slice. The times are simulated.
32 devices in a mesh: dp: 16 (over z, y, core), fsdp: 2 (over x).
Axes of the slice: x: 2, y: 2, z: 4, core: 2. Of those that a mesh axis runs over, the one named last changes fastest.
Arguments:
- tokens: bfloat16 [32768, 768], P(('dp', 'fsdp')), may hold values from -6 to 6
- segment_ids: int32 [32768], P(('dp', 'fsdp')), may hold values from 0 to 255, never falling along the last dimension, each value on 1 to 384 neighbouring positions
- cotangent: bfloat16 [32768, 768], P(('dp', 'fsdp')), may hold values from -6 to 6
- norm1_gain: float32 [768], P('fsdp'), may hold values from 0.5 to 1.5
- norm1_shift: float32 [768], P('fsdp'), may hold values from -1.75 to 1.75
- qkv_weight: float32 [768, 2304], P('fsdp'), may hold values from -0.21875 to 0.21875
- query_bias: float32 [768], P('fsdp'), may hold values from -3 to 3
- value_bias: float32 [768], P('fsdp'), may hold values from -3 to 3
- out_weight: float32 [768, 768], P('fsdp'), may hold values from -1.75 to 1.75
- out_bias: float32 [768], P('fsdp'), may hold values from -1.75 to 1.75
- norm2_gain: float32 [768], P('fsdp'), may hold values from 0.5 to 1.5
- norm2_shift: float32 [768], P('fsdp'), may hold values from -1.75 to 1.75
- up_weight: float32 [768, 3072], P('fsdp'), may hold values from -0.21875 to 0.21875
- up_bias: float32 [3072], P('fsdp'), may hold values from -3 to 3
- down_weight: float32 [3072, 768], P('fsdp'), may hold values from -0.109375 to 0.109375
- down_bias: float32 [768], P('fsdp'), may hold values from -1.75 to 1.75
Outputs:
- output: bfloat16 [32768, 768], P(('dp', 'fsdp'))
- input_grad: bfloat16 [32768, 768], P(('dp', 'fsdp'))
- norm1_gain_grad: float32 [768], P('fsdp')
- norm1_shift_grad: float32 [768], P('fsdp')
- qkv_weight_grad: float32 [768, 2304], P('fsdp')
- query_bias_grad: float32 [768], P('fsdp')
- value_bias_grad: float32 [768], P('fsdp')
- out_weight_grad: float32 [768, 768], P('fsdp')
- out_bias_grad: float32 [768], P('fsdp')
- norm2_gain_grad: float32 [768], P('fsdp')
- norm2_shift_grad: float32 [768], P('fsdp')
- up_weight_grad: float32 [768, 3072], P('fsdp')
- up_bias_grad: float32 [3072], P('fsdp')
- down_weight_grad: float32 [3072, 768], P('fsdp')
- down_bias_grad: float32 [768], P('fsdp')
Inputs may be any that keep to these rules, and one draw needn't show every extreme that they name: segment_ids never fall along the rows; each id covers 1 to 384 consecutive rows and some id covers exactly 384.
All inputs are finite; a program needn't handle non-finite values.
Results may differ from a plain program's by a relative error of at most 0.019.
Values may be sent and summed in bfloat16 or wider, within the bound.
A program may use at most 192 MiB of HBM per device.

v0:
```python
import jax
import jax.numpy as jnp
from jax import lax
from jax.sharding import PartitionSpec as P

HEADS = 12
SEQ = 512
EPSILON = 1e-06
LARGE_NEG = -1000000000.0


def layer_norm(inputs, gain_vec, shift_vec):
    centre = inputs - jnp.mean(inputs, -1, keepdims=True)
    spread = jnp.mean(centre * centre, -1, keepdims=True)
    return centre * lax.rsqrt(spread + EPSILON) * gain_vec + shift_vec


def gelu_exact(inputs):
    return jax.nn.gelu(inputs, approximate=False)


def matmul(left, right):
    return jnp.dot(left, right, preferred_element_type=jnp.float32)


def outer_sum(left, right):
    return jnp.einsum("ta,tb->ab", left, right, preferred_element_type=jnp.float32)


def back_mul(left, right):
    return jnp.einsum("tb,ab->ta", left, right, preferred_element_type=jnp.float32)


def column_sum(values_b):
    return jnp.sum(values_b.astype(jnp.float32), 0)


def scores_of(queries, key_rows, seg_block, scaling):
    raw_scores = jnp.einsum("qhd,khd->hqk", queries, key_rows, preferred_element_type=jnp.float32)
    allowed = seg_block[:, None] == seg_block[None, :]
    return jnp.where(allowed[None], raw_scores * scaling, LARGE_NEG)


def body(
    tokens,
    segment_ids,
    cotangent,
    norm1_gain,
    norm1_shift,
    qkv_weight,
    query_bias,
    value_bias,
    out_weight,
    out_bias,
    norm2_gain,
    norm2_shift,
    up_weight,
    up_bias,
    down_weight,
    down_bias,
):
    masters = [
        norm1_gain,
        norm1_shift,
        qkv_weight,
        query_bias,
        value_bias,
        out_weight,
        out_bias,
        norm2_gain,
        norm2_shift,
        up_weight,
        up_bias,
        down_weight,
        down_bias,
    ]
    rounded_params = [master.astype(jnp.bfloat16) for master in masters]
    fwd_params = (
        lax.all_gather(rounded_params[0], "fsdp", axis=0, tiled=True),
        lax.all_gather(rounded_params[1], "fsdp", axis=0, tiled=True),
        lax.all_gather(rounded_params[2], "fsdp", axis=0, tiled=True),
        lax.all_gather(rounded_params[3], "fsdp", axis=0, tiled=True),
        lax.all_gather(rounded_params[4], "fsdp", axis=0, tiled=True),
        lax.all_gather(rounded_params[5], "fsdp", axis=0, tiled=True),
        lax.all_gather(rounded_params[6], "fsdp", axis=0, tiled=True),
        lax.all_gather(rounded_params[7], "fsdp", axis=0, tiled=True),
        lax.all_gather(rounded_params[8], "fsdp", axis=0, tiled=True),
        lax.all_gather(rounded_params[9], "fsdp", axis=0, tiled=True),
        lax.all_gather(rounded_params[10], "fsdp", axis=0, tiled=True),
        lax.all_gather(rounded_params[11], "fsdp", axis=0, tiled=True),
        lax.all_gather(rounded_params[12], "fsdp", axis=0, tiled=True),
    )
    gain_one = fwd_params[0].astype(jnp.float32)
    shift_one = fwd_params[1].astype(jnp.float32)
    q_bias = fwd_params[3].astype(jnp.float32)
    v_bias = fwd_params[4].astype(jnp.float32)
    o_bias = fwd_params[6].astype(jnp.float32)
    gain_two = fwd_params[7].astype(jnp.float32)
    shift_two = fwd_params[8].astype(jnp.float32)
    u_bias = fwd_params[10].astype(jnp.float32)
    d_bias = fwd_params[12].astype(jnp.float32)
    rows_here = tokens.shape[0]
    width = tokens.shape[1]
    seq_here = rows_here // SEQ
    head_dim = width // HEADS
    scaling = head_dim ** (-0.5)
    seg_blocks = segment_ids.reshape(seq_here, SEQ)

    def attend_forward(block):
        queries, key_rows, value_rows, seg_block = block
        scores = scores_of(queries, key_rows, seg_block, scaling)
        row_max = jnp.max(scores, -1, keepdims=True)
        row_total = jnp.sum(jnp.exp(scores - row_max), -1, keepdims=True)
        log_total = row_max + jnp.log(row_total)
        attn_b = jnp.exp(scores - log_total).astype(jnp.bfloat16)
        att_out = jnp.einsum("hqk,khd->qhd", attn_b, value_rows, preferred_element_type=jnp.float32)
        return (att_out.astype(jnp.bfloat16), log_total)

    def attend_backward(block):
        queries, key_rows, value_rows, seg_block, log_total, grad_att = block
        scores = scores_of(queries, key_rows, seg_block, scaling)
        attn_f = jnp.exp(scores - log_total)
        attn_b = attn_f.astype(jnp.bfloat16)
        grad_values = jnp.einsum(
            "hqk,qhd->khd", attn_b, grad_att, preferred_element_type=jnp.float32
        )
        grad_attn = jnp.einsum(
            "qhd,khd->hqk", grad_att, value_rows, preferred_element_type=jnp.float32
        )
        row_dot = jnp.sum(grad_attn * attn_f, -1, keepdims=True)
        grad_scores = (attn_f * (grad_attn - row_dot)).astype(jnp.bfloat16)
        grad_queries = (
            jnp.einsum("hqk,khd->qhd", grad_scores, key_rows, preferred_element_type=jnp.float32)
            * scaling
        )
        grad_keys = (
            jnp.einsum("hqk,qhd->khd", grad_scores, queries, preferred_element_type=jnp.float32)
            * scaling
        )
        return (
            grad_queries.astype(jnp.bfloat16),
            grad_keys.astype(jnp.bfloat16),
            grad_values.astype(jnp.bfloat16),
        )

    inputs = tokens.astype(jnp.float32)
    normed_one, norm_one_pull = jax.vjp(layer_norm, inputs, gain_one, shift_one)
    act_one = normed_one.astype(jnp.bfloat16)
    linear = matmul(act_one, fwd_params[2]) + jnp.concatenate(
        [q_bias, jnp.zeros_like(q_bias), v_bias]
    )
    linear_b = linear.astype(jnp.bfloat16)
    queries = linear_b[:, :width].reshape(seq_here, SEQ, HEADS, head_dim)
    key_rows = linear_b[:, width : 2 * width].reshape(seq_here, SEQ, HEADS, head_dim)
    value_rows = linear_b[:, 2 * width :].reshape(seq_here, SEQ, HEADS, head_dim)
    attended, log_totals = lax.map(attend_forward, (queries, key_rows, value_rows, seg_blocks))
    attended = attended.reshape(rows_here, width)
    branch = matmul(attended, fwd_params[5]) + o_bias
    middle = inputs + branch
    normed_two, norm_two_pull = jax.vjp(layer_norm, middle, gain_two, shift_two)
    act_two = normed_two.astype(jnp.bfloat16)
    hidden_pre = matmul(act_two, fwd_params[9]) + u_bias
    gelu_out, gelu_pull = jax.vjp(gelu_exact, hidden_pre)
    hidden_b = gelu_out.astype(jnp.bfloat16)
    mlp_out = matmul(hidden_b, fwd_params[11]) + d_bias
    output = (middle + mlp_out).astype(jnp.bfloat16)
    back_params = (
        lax.all_gather(rounded_params[0], "fsdp", axis=0, tiled=True),
        lax.all_gather(rounded_params[1], "fsdp", axis=0, tiled=True),
        lax.all_gather(rounded_params[2], "fsdp", axis=0, tiled=True),
        lax.all_gather(rounded_params[3], "fsdp", axis=0, tiled=True),
        lax.all_gather(rounded_params[4], "fsdp", axis=0, tiled=True),
        lax.all_gather(rounded_params[5], "fsdp", axis=0, tiled=True),
        lax.all_gather(rounded_params[6], "fsdp", axis=0, tiled=True),
        lax.all_gather(rounded_params[7], "fsdp", axis=0, tiled=True),
        lax.all_gather(rounded_params[8], "fsdp", axis=0, tiled=True),
        lax.all_gather(rounded_params[9], "fsdp", axis=0, tiled=True),
        lax.all_gather(rounded_params[10], "fsdp", axis=0, tiled=True),
        lax.all_gather(rounded_params[11], "fsdp", axis=0, tiled=True),
        lax.all_gather(rounded_params[12], "fsdp", axis=0, tiled=True),
    )
    grad_out = cotangent.astype(jnp.float32)
    grad_wdown = outer_sum(hidden_b, cotangent)
    grad_dbias = jnp.sum(grad_out, 0)
    grad_hidden = back_mul(cotangent, back_params[11])
    grad_pre_b = gelu_pull(grad_hidden)[0].astype(jnp.bfloat16)
    grad_wup = outer_sum(act_two, grad_pre_b)
    grad_ubias = column_sum(grad_pre_b)
    grad_act_two = back_mul(grad_pre_b, back_params[9])
    grad_mid_norm, grad_gain_two, grad_shift_two = norm_two_pull(grad_act_two)
    grad_middle = grad_out + grad_mid_norm
    mlp_shards = (
        lax.psum_scatter(
            grad_wup.astype(jnp.bfloat16), "fsdp", scatter_dimension=0, tiled=True
        ).astype(jnp.float32),
        lax.psum_scatter(
            grad_ubias.astype(jnp.bfloat16), "fsdp", scatter_dimension=0, tiled=True
        ).astype(jnp.float32),
        lax.psum_scatter(
            grad_wdown.astype(jnp.bfloat16), "fsdp", scatter_dimension=0, tiled=True
        ).astype(jnp.float32),
        lax.psum_scatter(
            grad_dbias.astype(jnp.bfloat16), "fsdp", scatter_dimension=0, tiled=True
        ).astype(jnp.float32),
        lax.psum_scatter(
            grad_gain_two.astype(jnp.bfloat16), "fsdp", scatter_dimension=0, tiled=True
        ).astype(jnp.float32),
        lax.psum_scatter(
            grad_shift_two.astype(jnp.bfloat16), "fsdp", scatter_dimension=0, tiled=True
        ).astype(jnp.float32),
    )
    mlp_grads = (
        lax.psum(mlp_shards[0].astype(jnp.bfloat16), "dp").astype(jnp.float32),
        lax.psum(mlp_shards[1].astype(jnp.bfloat16), "dp").astype(jnp.float32),
        lax.psum(mlp_shards[2].astype(jnp.bfloat16), "dp").astype(jnp.float32),
        lax.psum(mlp_shards[3].astype(jnp.bfloat16), "dp").astype(jnp.float32),
        lax.psum(mlp_shards[4].astype(jnp.bfloat16), "dp").astype(jnp.float32),
        lax.psum(mlp_shards[5].astype(jnp.bfloat16), "dp").astype(jnp.float32),
    )
    grad_branch_b = grad_middle.astype(jnp.bfloat16)
    grad_wout = outer_sum(attended, grad_branch_b)
    grad_obias = column_sum(grad_branch_b)
    grad_att_b = back_mul(grad_branch_b, back_params[5]).astype(jnp.bfloat16)
    grad_att_b = grad_att_b.reshape(seq_here, SEQ, HEADS, head_dim)
    grad_q_b, grad_k_b, grad_v_b = lax.map(
        attend_backward, (queries, key_rows, value_rows, seg_blocks, log_totals, grad_att_b)
    )
    grad_q_b = grad_q_b.reshape(rows_here, width)
    grad_k_b = grad_k_b.reshape(rows_here, width)
    grad_v_b = grad_v_b.reshape(rows_here, width)
    grad_linear_b = jnp.concatenate([grad_q_b, grad_k_b, grad_v_b], 1)
    grad_wqkv = outer_sum(act_one, grad_linear_b)
    grad_qbias = column_sum(grad_q_b)
    grad_vbias = column_sum(grad_v_b)
    grad_act_one = back_mul(grad_linear_b, back_params[2])
    grad_in_norm, grad_gain_one, grad_shift_one = norm_one_pull(grad_act_one)
    input_grad = (grad_middle + grad_in_norm).astype(jnp.bfloat16)
    attn_shards = (
        lax.psum_scatter(
            grad_gain_one.astype(jnp.bfloat16), "fsdp", scatter_dimension=0, tiled=True
        ).astype(jnp.float32),
        lax.psum_scatter(
            grad_shift_one.astype(jnp.bfloat16), "fsdp", scatter_dimension=0, tiled=True
        ).astype(jnp.float32),
        lax.psum_scatter(
            grad_wqkv.astype(jnp.bfloat16), "fsdp", scatter_dimension=0, tiled=True
        ).astype(jnp.float32),
        lax.psum_scatter(
            grad_qbias.astype(jnp.bfloat16), "fsdp", scatter_dimension=0, tiled=True
        ).astype(jnp.float32),
        lax.psum_scatter(
            grad_vbias.astype(jnp.bfloat16), "fsdp", scatter_dimension=0, tiled=True
        ).astype(jnp.float32),
        lax.psum_scatter(
            grad_wout.astype(jnp.bfloat16), "fsdp", scatter_dimension=0, tiled=True
        ).astype(jnp.float32),
        lax.psum_scatter(
            grad_obias.astype(jnp.bfloat16), "fsdp", scatter_dimension=0, tiled=True
        ).astype(jnp.float32),
    )
    attn_grads = (
        lax.psum(attn_shards[0].astype(jnp.bfloat16), "dp").astype(jnp.float32),
        lax.psum(attn_shards[1].astype(jnp.bfloat16), "dp").astype(jnp.float32),
        lax.psum(attn_shards[2].astype(jnp.bfloat16), "dp").astype(jnp.float32),
        lax.psum(attn_shards[3].astype(jnp.bfloat16), "dp").astype(jnp.float32),
        lax.psum(attn_shards[4].astype(jnp.bfloat16), "dp").astype(jnp.float32),
        lax.psum(attn_shards[5].astype(jnp.bfloat16), "dp").astype(jnp.float32),
        lax.psum(attn_shards[6].astype(jnp.bfloat16), "dp").astype(jnp.float32),
    )
    return (
        output,
        input_grad,
        attn_grads[0],
        attn_grads[1],
        attn_grads[2],
        attn_grads[3],
        attn_grads[4],
        attn_grads[5],
        attn_grads[6],
        mlp_grads[4],
        mlp_grads[5],
        mlp_grads[0],
        mlp_grads[1],
        mlp_grads[2],
        mlp_grads[3],
    )


def solution(mesh):
    placed = (
        P(("dp", "fsdp"), None),
        P(("dp", "fsdp")),
        P(("dp", "fsdp"), None),
        P("fsdp"),
        P("fsdp"),
        P("fsdp", None),
        P("fsdp"),
        P("fsdp"),
        P("fsdp", None),
        P("fsdp"),
        P("fsdp"),
        P("fsdp"),
        P("fsdp", None),
        P("fsdp"),
        P("fsdp", None),
        P("fsdp"),
    )
    return jax.shard_map(
        body,
        mesh=mesh,
        in_specs=placed,
        out_specs=(
            P(("dp", "fsdp"), None),
            P(("dp", "fsdp"), None),
            P("fsdp"),
            P("fsdp"),
            P("fsdp", None),
            P("fsdp"),
            P("fsdp"),
            P("fsdp", None),
            P("fsdp"),
            P("fsdp"),
            P("fsdp"),
            P("fsdp", None),
            P("fsdp"),
            P("fsdp", None),
            P("fsdp"),
        ),
        check_vma=False,
    )
```

profile of v0, /device:TPU:0, one launch (start us, length us, event | category | flops | bytes accessed | tf_op | source)
XLA Modules:
  0.0 684.2 jit_solution(3355608891467746422)
XLA Ops:
  7.2 3.5 convert_element_type.236
  11.7 4.1 convert_element_type.250
  16.0 4.0 convert_element_type.254
  20.3 5.3 all-gather.6
  25.6 4.3 all-gather.5
  30.0 4.3 all-gather.4
  34.4 4.3 all-gather.3
  38.8 4.3 all-gather.2
  43.1 4.3 all-gather.1
  47.5 4.3 all-gather
  52.0 4.5 all-gather.7
  60.7 2.6 all-gather.14.cloned.1.call-done
  63.3 6.4 add_convert_fusion.1
  73.3 4.0 reshape.219
  80.7 3.8 reshape.218
  86.3 2.6 copy.84
  88.8 3.8 reshape.216
  92.7 2.9 copy.87
  96.9 20.6 %while.26 = (s32[]{:T(128)}, bf16[2,512,12,64]{1,3,2,0:T(8,128)(2,1)}, f32[2,12,512,1]{2,1,3,0:T(8,128)S(1)}, bf16[2,512,12,64]{1,3,2,0:T(8,128)(2,1)}, s32[2,51...) while((s32[]{:T(128)}, ...), condition=%wide.region_5.6_spmd, body=%wide.region_2.5_spmd.sunk | while | flops 840558592 | bytes 42180708 | solution.py:156
  99.7 2.6 exponential_reduce_fusion.2
  102.3 5.2 fusion.129
  109.8 2.6 exponential_reduce_fusion.2
  112.4 5.1 fusion.129
  117.5 4.2 copy.90
  123.3 3.8 fusion.86
  127.6 25.5 %all-gather.18.cloned.1.call-done = bf16[768,3072]{1,0:T(8,128)(2,1)} async-done(((bf16[384,3072]{1,0:T(8,128)(2,1)}), bf16[768,3072]{1,0:T(8,128)(2,1)}) %all-gather.18.cloned.1.call-update) | async-done | bytes 4718608 | tf_op jit(solution)/shard_map/all_gather | solution.py:88
  153.0 37.7 %multiply_convert_fusion.3 = (bf16[1024,3072]{1,0:T(8,128)(2,1)}, f32[1024,3072]{1,0:T(8,128)}, f32[1024,3072]{1,0:T(8,128)}) fusion(f32[3072]{0:T(1024)S(1)} %bitcast.168, bf16[768,3072]{1,0:T(8,128)(2,1)} %all-gather.18.cloned.1.call-done, f32[1024,768]{0,1:T(8,128)S(1)} %get-tuple-element.284, f32[768]{0:T(1024)S(1)} %reshape.249, ...), kind=kOutput, calls=%fused_computation.68 | convolution fusion | flops 5043388416 | bytes 39348224 | tf_op jit(solution)/shard_map/dot_general | solution.py:23
  190.8 26.9 %all-gather.20.cloned.1.call-done = bf16[3072,768]{1,0:T(8,128)(2,1)} async-done(((bf16[1536,768]{1,0:T(8,128)(2,1)}), bf16[3072,768]{1,0:T(8,128)(2,1)}) %all-gather.20.cloned.1.call-update) | async-done | bytes 4718608 | tf_op jit(solution)/shard_map/all_gather | solution.py:90
  217.7 18.9 %fusion.89 = (bf16[3072]{0:T(1024)(128)(2,1)}, bf16[1024,3072]{1,0:T(8,128)(2,1)}) fusion(f32[1024,3072]{1,0:T(8,128)} %get-tuple-element.275, bf16[1024,768]{1,0:T(8,128)(2,1)} %param.22, bf16[3072,768]{1,0:T(8,128)(2,1)} %all-gather.20.cloned.1.call-done, f32[1024,3072]{1,0:T(8,128)} %get-tuple-element.285, f32[3072]{0:T(1024)S(1)} %bitcast.169), kind=kOutput, calls=%fused_computation.142 | convolution fusion | flops 4882166784 | bytes 37767168 | tf_op jit(solution)/shard_map/tb,ab->ta/dot_general | solution.py:31
  236.6 10.3 %fusion.88 = (bf16[768]{0:T(1024)(128)(2,1)}, f32[1024,768]{1,0:T(8,128)}) fusion(bf16[1024,3072]{1,0:T(8,128)(2,1)} %get-tuple-element.291, bf16[768,3072]{1,0:T(8,128)(2,1)} %all-gather.18.cloned.1.call-done), kind=kOutput, calls=%fused_computation.141 | convolution fusion | flops 4832623616 | bytes 14157312 | tf_op jit(solution)/shard_map/tb,ab->ta/dot_general | solution.py:31
  246.9 3.5 copy.93
  250.5 3.5 multiply_reduce_fusion.1
  257.5 2.4 convolution_convert_fusion.4
  260.0 2.7 convolution_convert_fusion.3
  270.5 49.0 %while.27 = (s32[]{:T(128)}, bf16[2,512,12,64]{1,3,2,0:T(8,128)(2,1)}, bf16[2,512,12,64]{1,3,2,0:T(8,128)(2,1)}, bf16[2,512,12,64]{1,3,2,0:T(8,128)(2,1)}, bf16[...) while((s32[]{:T(128)}, ...), condition=%wide.region_12.13_spmd, body=%wide.region_10.12_spmd.sunk | while | flops 2062673920 | bytes 141233456 | solution.py:225
  272.7 4.0 fusion.141
  276.6 6.9 %multiply_reduce_fusion.5 = (f32[12,512]{1,0:T(8,128)S(1)}, f32[12,512,512]{1,2,0:T(8,128)}) fusion(f32[12,512,512]{1,2,0:T(8,128)S(1)} %fusion.138, f32[12,512]{1,0:T(8,128)S(1)} %dynamic-slice_bitcast_fusion.2, pred[512,512]{0,1:T(8,128)(4,1)S(1)} %broadcast_compare_fusion.5, bf16[2,512,12,64]{1,3,2,0:T(8,128)(2,1)S(1)} %copy-done.10, ...), kind=kOutput, calls=%fused_computation.25.clone.1 | convolution fusion | flops 418375680 | bytes 27059200 | tf_op jit(solution)/shard_map/while/body/eval_jaxpr/qhd,khd->hqk/dot_general | solution.py:127
  283.5 7.1 %multiply_convert_fusion.5 = bf16[12,512,512]{1,2,0:T(8,128)(2,1)S(1)} fusion(f32[12,512,512]{1,2,0:T(8,128)} %get-tuple-element.406, f32[12,512,512]{1,2,0:T(8,128)S(1)} %fusion.138, f32[12,512]{1,0:T(8,128)S(1)} %get-tuple-element.407, f32[12,512]{1,0:T(8,128)S(1)} %dynamic-slice_bitcast_fusion.2, pred[512,512]{0,1:T(8,128)(4,1)S(1)} %broadcast_compare_fusion.5), kind=kLoop, calls=%fused_computation.24.clone.1 | loop fusion | flops 18874368 | bytes 31768576 | tf_op jit(solution)/shard_map/while/body/eval_jaxpr/convert_element_type | solution.py:131
  297.1 3.9 fusion.141
  301.0 6.9 %multiply_reduce_fusion.5 = (f32[12,512]{1,0:T(8,128)S(1)}, f32[12,512,512]{1,2,0:T(8,128)}) fusion(f32[12,512,512]{1,2,0:T(8,128)S(1)} %fusion.138, f32[12,512]{1,0:T(8,128)S(1)} %dynamic-slice_bitcast_fusion.2, pred[512,512]{0,1:T(8,128)(4,1)S(1)} %broadcast_compare_fusion.5, bf16[2,512,12,64]{1,3,2,0:T(8,128)(2,1)S(1)} %copy-done.10, ...), kind=kOutput, calls=%fused_computation.25.clone.1 | convolution fusion | flops 418375680 | bytes 27059200 | tf_op jit(solution)/shard_map/while/body/eval_jaxpr/qhd,khd->hqk/dot_general | solution.py:127
  307.9 7.1 %multiply_convert_fusion.5 = bf16[12,512,512]{1,2,0:T(8,128)(2,1)S(1)} fusion(f32[12,512,512]{1,2,0:T(8,128)} %get-tuple-element.406, f32[12,512,512]{1,2,0:T(8,128)S(1)} %fusion.138, f32[12,512]{1,0:T(8,128)S(1)} %get-tuple-element.407, f32[12,512]{1,0:T(8,128)S(1)} %dynamic-slice_bitcast_fusion.2, pred[512,512]{0,1:T(8,128)(4,1)S(1)} %broadcast_compare_fusion.5), kind=kLoop, calls=%fused_computation.24.clone.1 | loop fusion | flops 18874368 | bytes 31768576 | tf_op jit(solution)/shard_map/while/body/eval_jaxpr/convert_element_type | solution.py:131
  319.5 3.0 copy.100
  323.0 3.1 copy.101
  331.2 5.7 convolution_convert_fusion.2
  337.0 9.1 %convolution_convert_fusion = bf16[3072,768]{1,0:T(8,128)(2,1)} fusion(bf16[1024,3072]{1,0:T(8,128)(2,1)} %get-tuple-element.274, bf16[1024,768]{1,0:T(8,128)(2,1)} %param.22), kind=kOutput, calls=%fused_computation.83 | convolution fusion | flops 4834197504 | bytes 12582912 | tf_op jit(solution)/shard_map/ta,tb->ab/dot_general | solution.py:27
  346.8 9.9 %convolution_convert_fusion.1 = bf16[768,3072]{1,0:T(8,128)(2,1)} fusion(bf16[1024,3072]{1,0:T(8,128)(2,1)} %get-tuple-element.291, f32[1024,768]{0,1:T(8,128)} %copy-done.7, f32[768]{0:T(1024)S(1)} %copy-done.51, f32[768]{0:T(1024)S(1)} %copy-done.43, f32[1024]{0:T(1024)S(1)} %copy-done.45, f32[1024]{0:T(1024)S(1)} %copy-done.35), kind=kOutput, calls=%fused_computation.84 | convolution fusion | flops 4838129664 | bytes 14170112 | tf_op jit(solution)/shard_map/ta,tb->ab/dot_general | solution.py:27
  359.3 4.3 all-gather.8
  365.4 19.4 %reduce-scatter.5.cloned.1.call-done = bf16[384,2304]{1,0:T(8,128)(2,1)} async-done(((bf16[768,2304]{1,0:T(8,128)(2,1)}), bf16[384,2304]{1,0:T(8,128)(2,1)}) %reduce-scatter.5.cloned.1.call-update) | async-done | bytes 1769488 | tf_op jit(solution)/shard_map/reduce_scatter | solution.py:245
  384.8 62.3 %reduce-scatter.11.cloned.1.call-done = bf16[1536,768]{1,0:T(8,128)(2,1)} async-done(((bf16[3072,768]{1,0:T(8,128)(2,1)}), bf16[1536,768]{1,0:T(8,128)(2,1)}) %reduce-scatter.11.cloned.1.call-update) | async-done | bytes 2359312 | tf_op jit(solution)/shard_map/reduce_scatter | solution.py:199
  447.1 63.0 %reduce-scatter.9.cloned.1.call-done = bf16[384,3072]{1,0:T(8,128)(2,1)} async-done(((bf16[768,3072]{1,0:T(8,128)(2,1)}), bf16[384,3072]{1,0:T(8,128)(2,1)}) %reduce-scatter.9.cloned.1.call-update) | async-done | bytes 2359312 | tf_op jit(solution)/shard_map/reduce_scatter | solution.py:193
  510.2 10.0 %add_convert_fusion.3 = bf16[1024,768]{0,1:T(8,128)(2,1)} fusion(f32[1024,768]{0,1:T(8,128)} %copy-done.7, bf16[1024,3072]{1,0:T(8,128)(2,1)} %get-tuple-element.274, bf16[3072,768]{1,0:T(8,128)(2,1)} %all-gather.20.cloned.1.call-done, f32[768]{0:T(1024)S(1)} %reshape.251), kind=kOutput, calls=%fused_computation.106 | convolution fusion | flops 4834197504 | bytes 15731712 | tf_op jit(solution)/shard_map/dot_general | solution.py:23
  520.1 2.6 copy.105
  524.9 9.1 %fusion.87 = (bf16[768]{0:T(1024)(128)(2,1)S(1)}, f32[1024,768]{1,0:T(8,128)}) fusion(bf16[1024,2304]{0,1:T(8,128)(2,1)} %copy-done.25, bf16[768,2304]{1,0:T(8,128)(2,1)} %all-gather.14.cloned.1.call-done), kind=kOutput, calls=%fused_computation.140 | convolution fusion | flops 3624664320 | bytes 11404800 | tf_op jit(solution)/shard_map/tb,ab->ta/dot_general | solution.py:31
  534.0 3.6 copy.102
  537.6 2.6 fusion.73
  541.9 7.4 %all-reduce.11 = (bf16[768]{0:T(1024)(128)(2,1)S(1)}, bf16[768]{0:T(1024)(128)(2,1)S(1)}, bf16[768]{0:T(1024)(128)(2,1)S(1)}, bf16[768]{0:T(1024)(128)(2,1)S(1)}...) all-reduce(bf16[768]{0:T(1024)(128)(2,1)S(1)} %get-tuple-element.21, ...), channel_id=2, replica_groups=mesh['dp'=16,'fsdp'=2] {'fsdp'}, use_global_device_ids=true, to_apply=%region_16.17.clone | all-reduce | flops 9216 | bytes 36864
  550.0 61.8 %all-reduce.9 = (bf16[384]{0:T(512)(128)(2,1)S(1)}, bf16[384]{0:T(512)(128)(2,1)S(1)}, bf16[384]{0:T(512)(128)(2,1)S(1)}, bf16[384]{0:T(512)(128)(2,1)S(1)}, bf1...) all-reduce(bf16[384]{0:T(512)(128)(2,1)S(1)} %dynamic-slice.1, ...), channel_id=1, replica_groups=mesh['dp'=16,'fsdp'=2] {'dp'}, use_global_device_ids=true, to_apply=%region_17.18 | all-reduce | flops 4608 | bytes 18432 | tf_op jit(solution)/shard_map/psum | solution.py:262
  616.5 6.2 add_convert_fusion.2
  622.7 2.6 copy.106
  625.9 40.3 %all-reduce.14.cloned.1.call-done = (bf16[384,2304]{1,0:T(8,128)(2,1)}, bf16[384,768]{1,0:T(8,128)(2,1)}, bf16[384,3072]{1,0:T(8,128)(2,1)}, bf16[1536,768]{1,0:T(8,128)(2,1)}) async-done(((bf16[384,2304]{1,0:T(8,128)(2,1)}, bf16[384,768]{1,0:T(8,128)(2,1)}, bf16[384,3072]{1,0:T(8,128)(2,1)}, bf16[1536,768]{1,0:T(8,128)(2,1)}), (bf16[384,2304]{1,0:T(8,128)(2,1)}, bf16[384,768]{1,0:T(8,128)(2,1)}, ...) | async-done | bytes 7077904 | tf_op jit(solution)/shard_map/psum | solution.py:264
  666.2 2.3 convert_element_type.272
  668.5 3.5 convert_element_type.268
  672.0 2.8 convert_element_type.279
  674.7 2.5 convert_element_type.282
  (282 shorter events, 65.2 us)
Async XLA Ops:
  7.2 3.6 copy-start.24
  7.2 56.1 %all-gather.14.cloned.1.call-start = ((), (), s32[]{:S(2)}) async-start(), calls=%async_computation.4 | async-start | bytes 5308416 | tf_op jit(solution)/shard_map/all_gather | solution.py:81
  10.7 112.6 %all-gather.16.cloned.1.call-start = ((), (), s32[]{:S(2)}) async-start(), calls=%async_computation.5 | async-start | bytes 1769472 | tf_op jit(solution)/shard_map/all_gather | solution.py:84
  11.7 141.4 %all-gather.18.cloned.1.call-start = ((), (), s32[]{:S(2)}) async-start(), calls=%async_computation.6 | async-start | bytes 7077888 | tf_op jit(solution)/shard_map/all_gather | solution.py:88
  15.8 4.2 copy-start.55
  15.9 4.2 copy-start.56
  15.9 4.3 copy-start.57
  15.9 4.3 copy-start.58
  15.9 4.3 copy-start.59
  15.9 4.3 copy-start.60
  15.9 4.3 copy-start.61
  15.9 36.0 %copy-start.54 = (s32[1024]{0:T(1024)S(1)}, s32[1024]{0:T(1024)}, u32[]{:S(2)}) copy-start(s32[1024]{0:T(1024)} %param.21) | copy-start | bytes 12292
  15.9 36.0 %copy-start.48 = (f32[1536]{0:T(1024)S(1)}, f32[1536]{0:T(1024)}, u32[]{:S(2)}) copy-start(f32[1536]{0:T(1024)} %param.33) | copy-start | bytes 18436
  16.0 201.8 %all-gather.20.cloned.1.call-start = ((), (), s32[]{:S(2)}) async-start(), calls=%async_computation.7 | async-start | bytes 7077888 | tf_op jit(solution)/shard_map/all_gather | solution.py:90
  20.0 345.4 %reduce-scatter.7.cloned.1.call-start = ((), (), s32[]{:S(2)}) async-start(), calls=%async_computation.9 | async-start | bytes 1769472 | tf_op jit(solution)/shard_map/reduce_scatter | solution.py:254
  25.6 127.4 %copy-start.50 = (f32[768]{0:T(1024)}, f32[768]{0:T(1024)S(1)}, u32[]{:S(2)}) copy-start(f32[768]{0:T(1024)S(1)} %reshape.249) | copy-start | bytes 9220
  30.0 224.0 %copy-start.42 = (f32[768]{0:T(1024)}, f32[768]{0:T(1024)S(1)}, u32[]{:S(2)}) copy-start(f32[768]{0:T(1024)S(1)} %reshape.248) | copy-start | bytes 9220
  47.5 15.8 %copy-start.52 = (f32[768]{0:T(1024)}, f32[768]{0:T(1024)S(1)}, u32[]{:S(2)}) copy-start(f32[768]{0:T(1024)S(1)} %reshape.244) | copy-start | bytes 9220
  51.9 11.4 %copy-start.32 = (f32[768]{0:T(1024)}, f32[768]{0:T(1024)S(1)}, u32[]{:S(2)}) copy-start(f32[768]{0:T(1024)S(1)} %reshape.243) | copy-start | bytes 9220
  56.4 2.6 copy-start.17
  58.3 11.4 %copy-start.4 = (bf16[1024,768]{0,1:T(8,128)(2,1)}, bf16[1024,768]{0,1:T(8,128)(2,1)S(1)}, u32[]{:S(2)}) copy-start(bf16[1024,768]{0,1:T(8,128)(2,1)S(1)} %copy.83) | copy-start | bytes 4718596
  58.6 11.1 %copy-start.30 = (f32[1024]{0:T(1024)}, f32[1024]{0:T(1024)S(1)}, u32[]{:S(2)}) copy-start(f32[1024]{0:T(1024)S(1)} %broadcast_multiply_fusion.1) | copy-start | bytes 12292
  59.0 10.7 %copy-start.40 = (f32[1024]{0:T(1024)}, f32[1024]{0:T(1024)S(1)}, u32[]{:S(2)}) copy-start(f32[1024]{0:T(1024)S(1)} %fusion.72) | copy-start | bytes 12292
  59.1 10.6 %copy-start.36 = (f32[1024]{0:T(1024)}, f32[1024]{0:T(1024)S(1)}, u32[]{:S(2)}) copy-start(f32[1024]{0:T(1024)S(1)} %fusion.76) | copy-start | bytes 12292
  73.3 5.8 copy-start.18
  117.5 5.8 copy-start
  117.5 5.8 copy-start.2
  117.5 5.8 copy-start.26
  117.5 5.8 copy-start.28
  127.1 126.9 %copy-start.7 = (f32[1024,768]{0,1:T(8,128)}, f32[1024,768]{0,1:T(8,128)S(1)}, u32[]{:S(2)}) copy-start(f32[1024,768]{0,1:T(8,128)S(1)} %get-tuple-element.284) | copy-start | bytes 9437188
  127.1 126.9 %copy-start.34 = (f32[1024]{0:T(1024)}, f32[1024]{0:T(1024)S(1)}, u32[]{:S(2)}) copy-start(f32[1024]{0:T(1024)S(1)} %broadcast_multiply_fusion) | copy-start | bytes 12292
  127.5 126.5 %copy-start.44 = (f32[1024]{0:T(1024)}, f32[1024]{0:T(1024)S(1)}, u32[]{:S(2)}) copy-start(f32[1024]{0:T(1024)S(1)} %fusion.77) | copy-start | bytes 12292
  250.5 3.5 copy-start.8
  255.5 2.0 copy-start.23
  259.9 124.9 %reduce-scatter.5.cloned.1.call-start = ((), (), s32[]{:S(2)}) async-start(), calls=%async_computation.8 | async-start | bytes 5308416 | tf_op jit(solution)/shard_map/reduce_scatter | solution.py:245
  266.5 4.0 copy-start.1
  266.5 4.0 copy-start.3
  266.5 4.0 copy-start.27
  266.5 4.0 copy-start.29
  270.8 1.9 copy-start.11
  272.6 4.0 copy-start.10
  283.5 7.1 %copy-start.19 = (bf16[2,512,12,64]{1,3,2,0:T(8,128)(2,1)S(1)}, bf16[2,512,12,64]{1,3,2,0:T(8,128)(2,1)}, u32[]{:S(2)}) copy-start(bf16[2,512,12,64]{1,3,2,0:T(8,128)(2,1)} %get-tuple-element.445) | copy-start | bytes 4718596 | tf_op jit(solution)/shard_map/while
  290.6 2.0 copy-start.14
  295.2 1.9 copy-start.11
  297.1 4.0 copy-start.10
  307.9 7.1 %copy-start.19 = (bf16[2,512,12,64]{1,3,2,0:T(8,128)(2,1)S(1)}, bf16[2,512,12,64]{1,3,2,0:T(8,128)(2,1)}, u32[]{:S(2)}) copy-start(bf16[2,512,12,64]{1,3,2,0:T(8,128)(2,1)} %get-tuple-element.445) | copy-start | bytes 4718596 | tf_op jit(solution)/shard_map/while
  315.0 2.0 copy-start.14
  322.9 3.6 copy-start.16
  328.7 2.5 copy-start.5
  328.7 2.5 copy-start.31
  328.7 2.5 copy-start.33
  328.7 2.5 copy-start.37
  328.7 2.5 copy-start.53
  329.0 2.2 copy-start.25
  336.9 110.2 %reduce-scatter.11.cloned.1.call-start = ((), (), s32[]{:S(2)}) async-start(), calls=%async_computation.11 | async-start | bytes 7077888 | tf_op jit(solution)/shard_map/reduce_scatter | solution.py:199
  346.2 164.0 %reduce-scatter.9.cloned.1.call-start = ((), (), s32[]{:S(2)}) async-start(), calls=%async_computation.10 | async-start | bytes 7077888 | tf_op jit(solution)/shard_map/reduce_scatter | solution.py:193
  356.8 2.5 copy-start.62
  356.8 309.4 %all-reduce.14.cloned.1.call-start = ((), (), s32[]{:S(2)}) async-start(), calls=%async_computation.12 | async-start | bytes 14155776 | tf_op jit(solution)/shard_map/psum | solution.py:264
  537.6 2.6 copy-start.41
  537.6 3.0 copy-start.6
  540.3 76.2 %copy-start.13 = (bf16[1024,768]{0,1:T(8,128)(2,1)S(1)}, bf16[1024,768]{0,1:T(8,128)(2,1)}, u32[]{:S(2)}) copy-start(bf16[1024,768]{0,1:T(8,128)(2,1)} %copy.92) | copy-start | bytes 4718596
  540.3 76.2 %copy-start.39 = (f32[1024]{0:T(1024)S(1)}, f32[1024]{0:T(1024)}, u32[]{:S(2)}) copy-start(f32[1024]{0:T(1024)} %copy-done.38) | copy-start | bytes 12292
  666.2 5.8 copy-start.22
  672.0 2.8 copy-start.21
  (16 other events, 19.4 us)
Sparse Core Ops, SparseCore 0:
  10.8 52.3 all-gather.13
  65.4 22.7 all-gather.15
  90.4 62.6 all-gather.17
  155.0 62.6 all-gather.19
  260.0 21.7 reduce-scatter.6
  337.1 47.6 reduce-scatter.4
  387.1 59.9 reduce-scatter.10
  450.1 59.9 reduce-scatter.8
  514.2 151.9 all-reduce.13
where the time goes:
time: 692 us; the launch traced here: 684 us
  waiting for transfers between devices  240 us (35%)
  matrix products  172 us (25%)
  blocking collectives  109 us (16%)
  local copies, waits for them, and re-layouts  75 us (11%)
  other arithmetic  69.7 us (10%)
  between operations  16.6 us (2%)
    reduce_scatter x1, waiting for transfers between devices, body(): lax.psum_scatter(grad_wup.astype(jnp.bfloat16), 'fsdp', scatter_dimension...  63 us
    reduce_scatter x1, waiting for transfers between devices, body(): lax.psum_scatter(grad_wdown.astype(jnp.bfloat16), 'fsdp', scatter_dimensi...  62.3 us
    psum x1, blocking collectives, body(): lax.psum(attn_shards[0].astype(jnp.bfloat16), 'dp').astype(jnp.float32)  61.8 us
    dot_general x4, matrix products, matmul(): return jnp.dot(left, right, preferred_element_type=jnp.float32)  57.9 us
    dot_general x4, matrix products, back_mul(): jnp.einsum('tb,ab->ta', left, right, preferred_element_type=jnp.float32)  41.1 us
    psum x1, waiting for transfers between devices, body(): lax.psum(attn_shards[2].astype(jnp.bfloat16), 'dp').astype(jnp.float32)  40.3 us
    dot_general x4, matrix products, outer_sum(): jnp.einsum('ta,tb->ab', left, right, preferred_element_type=jnp.float32)  27.2 us
    all_gather x1, waiting for transfers between devices, body(): lax.all_gather(rounded_params[11], 'fsdp', axis=0, tiled=True)  26.9 us
  transfers between devices with their start and end apart: 9, of which 7 were waited for; matrix products, arithmetic and copies ran while one was open for 37% of the time, Pallas kernels for 0%

commit v1 on v0

--- a/solution.py
+++ b/solution.py
@@ -259,7 +259,9 @@
         ).astype(jnp.float32),
     )
     attn_grads = (
-        lax.psum(attn_shards[0].astype(jnp.bfloat16), "dp").astype(jnp.float32),
+        jnp.sum(lax.all_gather(attn_shards[0].astype(jnp.bfloat16), "dp"), axis=0).astype(
+            jnp.float32
+        ),
         lax.psum(attn_shards[1].astype(jnp.bfloat16), "dp").astype(jnp.float32),
         lax.psum(attn_shards[2].astype(jnp.bfloat16), "dp").astype(jnp.float32),
         lax.psum(attn_shards[3].astype(jnp.bfloat16), "dp").astype(jnp.float32),

time: 692 us -> 692 us (level)
  blocking collectives: 109 us -> 127 us
  waiting for transfers between devices: 240 us -> 223 us
    all_gather x0 -> x1, blocking collectives: none -> 17.5 us  [body(): lax.all_gather(attn_shards[0].astype(jnp.bfloat16), 'dp')]
    psum x1, waiting for transfers between devices: 40.3 us -> 23 us  [body(): lax.psum(attn_shards[2].astype(jnp.bfloat16), 'dp').astype(jnp.float32)]
    unnamed x147 -> x148, local copies, waits for them, and re-layouts: 18.2 us -> 18.2 us
where the time goes in v1:
time: 692 us; the launch traced here: 684 us
  waiting for transfers between devices  223 us (32%)
  matrix products  172 us (25%)
  blocking collectives  127 us (18%)
  local copies, waits for them, and re-layouts  75 us (11%)
  other arithmetic  69.6 us (10%)
  between operations  16.6 us (2%)
    reduce_scatter x1, waiting for transfers between devices, body(): lax.psum_scatter(grad_wup.astype(jnp.bfloat16), 'fsdp', scatter_dimension...  63 us
    reduce_scatter x1, waiting for transfers between devices, body(): lax.psum_scatter(grad_wdown.astype(jnp.bfloat16), 'fsdp', scatter_dimensi...  62.3 us
    psum x1, blocking collectives, body(): lax.psum(attn_shards[1].astype(jnp.bfloat16), 'dp').astype(jnp.float32)  61.8 us
    dot_general x4, matrix products, matmul(): return jnp.dot(left, right, preferred_element_type=jnp.float32)  57.8 us
    dot_general x4, matrix products, back_mul(): jnp.einsum('tb,ab->ta', left, right, preferred_element_type=jnp.float32)  41.1 us
    dot_general x4, matrix products, outer_sum(): jnp.einsum('ta,tb->ab', left, right, preferred_element_type=jnp.float32)  27.2 us
    all_gather x1, waiting for transfers between devices, body(): lax.all_gather(rounded_params[11], 'fsdp', axis=0, tiled=True)  27 us
    all_gather x1, waiting for transfers between devices, body(): lax.all_gather(rounded_params[9], 'fsdp', axis=0, tiled=True)  25.5 us
  transfers between devices with their start and end apart: 9, of which 7 were waited for; matrix products, arithmetic and copies ran while one was open for 37% of the time, Pallas kernels for 0%

profile of v1, /device:TPU:0, one launch (start us, length us, event | category | flops | bytes accessed | tf_op | source)
XLA Modules:
  0.0 684.3 jit_solution(10078024031572251950)
XLA Ops:
  7.2 3.5 convert_element_type.238
  11.7 4.1 convert_element_type.252
  16.0 4.0 convert_element_type.256
  20.3 5.3 all-gather.7
  25.6 4.3 all-gather.6
  30.0 4.3 all-gather.5
  34.4 4.3 all-gather.4
  38.8 4.3 all-gather.3
  43.1 4.3 all-gather.2
  47.5 4.3 all-gather.1
  52.0 4.5 all-gather.8
  60.7 2.5 all-gather.16.cloned.1.call-done
  63.3 6.4 add_convert_fusion.1
  73.3 4.0 reshape.219
  80.7 3.8 reshape.218
  86.3 2.6 copy.84
  88.9 3.8 reshape.216
  92.7 2.9 copy.87
  96.9 20.6 %while.26 = (s32[]{:T(128)}, bf16[2,512,12,64]{1,3,2,0:T(8,128)(2,1)}, f32[2,12,512,1]{2,1,3,0:T(8,128)S(1)}, bf16[2,512,12,64]{1,3,2,0:T(8,128)(2,1)}, s32[2,51...) while((s32[]{:T(128)}, ...), condition=%wide.region_5.6_spmd, body=%wide.region_2.5_spmd.sunk | while | flops 840558592 | bytes 42180708 | solution.py:156
  99.7 2.6 exponential_reduce_fusion.2
  102.3 5.2 fusion.129
  109.8 2.6 exponential_reduce_fusion.2
  112.4 5.1 fusion.129
  117.5 4.2 copy.90
  123.3 3.8 fusion.86
  127.6 25.5 %all-gather.20.cloned.1.call-done = bf16[768,3072]{1,0:T(8,128)(2,1)} async-done(((bf16[384,3072]{1,0:T(8,128)(2,1)}), bf16[768,3072]{1,0:T(8,128)(2,1)}) %all-gather.20.cloned.1.call-update) | async-done | bytes 4718608 | tf_op jit(solution)/shard_map/all_gather | solution.py:88
  153.0 37.6 %multiply_convert_fusion.3 = (bf16[1024,3072]{1,0:T(8,128)(2,1)}, f32[1024,3072]{1,0:T(8,128)}, f32[1024,3072]{1,0:T(8,128)}) fusion(f32[3072]{0:T(1024)S(1)} %bitcast.168, bf16[768,3072]{1,0:T(8,128)(2,1)} %all-gather.20.cloned.1.call-done, f32[1024,768]{0,1:T(8,128)S(1)} %get-tuple-element.283, f32[768]{0:T(1024)S(1)} %reshape.252, ...), kind=kOutput, calls=%fused_computation.68 | convolution fusion | flops 5043388416 | bytes 39348224 | tf_op jit(solution)/shard_map/dot_general | solution.py:23
  190.7 27.0 %all-gather.22.cloned.1.call-done = bf16[3072,768]{1,0:T(8,128)(2,1)} async-done(((bf16[1536,768]{1,0:T(8,128)(2,1)}), bf16[3072,768]{1,0:T(8,128)(2,1)}) %all-gather.22.cloned.1.call-update) | async-done | bytes 4718608 | tf_op jit(solution)/shard_map/all_gather | solution.py:90
  217.7 18.9 %fusion.89 = (bf16[3072]{0:T(1024)(128)(2,1)}, bf16[1024,3072]{1,0:T(8,128)(2,1)}) fusion(f32[1024,3072]{1,0:T(8,128)} %get-tuple-element.274, bf16[1024,768]{1,0:T(8,128)(2,1)} %param.22, bf16[3072,768]{1,0:T(8,128)(2,1)} %all-gather.22.cloned.1.call-done, f32[1024,3072]{1,0:T(8,128)} %get-tuple-element.284, f32[3072]{0:T(1024)S(1)} %bitcast.169), kind=kOutput, calls=%fused_computation.142 | convolution fusion | flops 4882166784 | bytes 37767168 | tf_op jit(solution)/shard_map/tb,ab->ta/dot_general | solution.py:31
  236.6 10.3 %fusion.88 = (bf16[768]{0:T(1024)(128)(2,1)}, f32[1024,768]{1,0:T(8,128)}) fusion(bf16[1024,3072]{1,0:T(8,128)(2,1)} %get-tuple-element.290, bf16[768,3072]{1,0:T(8,128)(2,1)} %all-gather.20.cloned.1.call-done), kind=kOutput, calls=%fused_computation.141 | convolution fusion | flops 4832623616 | bytes 14157312 | tf_op jit(solution)/shard_map/tb,ab->ta/dot_general | solution.py:31
  246.9 3.5 copy.93
  250.5 3.5 multiply_reduce_fusion.1
  257.5 2.4 convolution_convert_fusion.4
  260.0 2.7 convolution_convert_fusion.3
  270.5 49.0 %while.27 = (s32[]{:T(128)}, bf16[2,512,12,64]{1,3,2,0:T(8,128)(2,1)}, bf16[2,512,12,64]{1,3,2,0:T(8,128)(2,1)}, bf16[2,512,12,64]{1,3,2,0:T(8,128)(2,1)}, bf16[...) while((s32[]{:T(128)}, ...), condition=%wide.region_12.13_spmd, body=%wide.region_10.12_spmd.sunk | while | flops 2062673920 | bytes 141233456 | solution.py:225
  272.7 3.9 fusion.141
  276.6 6.9 %multiply_reduce_fusion.5 = (f32[12,512]{1,0:T(8,128)S(1)}, f32[12,512,512]{1,2,0:T(8,128)}) fusion(f32[12,512,512]{1,2,0:T(8,128)S(1)} %fusion.138, f32[12,512]{1,0:T(8,128)S(1)} %dynamic-slice_bitcast_fusion.2, pred[512,512]{0,1:T(8,128)(4,1)S(1)} %broadcast_compare_fusion.5, bf16[2,512,12,64]{1,3,2,0:T(8,128)(2,1)S(1)} %copy-done.10, ...), kind=kOutput, calls=%fused_computation.25.clone.1 | convolution fusion | flops 418375680 | bytes 27059200 | tf_op jit(solution)/shard_map/while/body/eval_jaxpr/qhd,khd->hqk/dot_general | solution.py:127
  283.5 7.1 %multiply_convert_fusion.5 = bf16[12,512,512]{1,2,0:T(8,128)(2,1)S(1)} fusion(f32[12,512,512]{1,2,0:T(8,128)} %get-tuple-element.405, f32[12,512,512]{1,2,0:T(8,128)S(1)} %fusion.138, f32[12,512]{1,0:T(8,128)S(1)} %get-tuple-element.406, f32[12,512]{1,0:T(8,128)S(1)} %dynamic-slice_bitcast_fusion.2, pred[512,512]{0,1:T(8,128)(4,1)S(1)} %broadcast_compare_fusion.5), kind=kLoop, calls=%fused_computation.24.clone.1 | loop fusion | flops 18874368 | bytes 31768576 | tf_op jit(solution)/shard_map/while/body/eval_jaxpr/convert_element_type | solution.py:131
  297.1 3.9 fusion.141
  301.0 6.9 %multiply_reduce_fusion.5 = (f32[12,512]{1,0:T(8,128)S(1)}, f32[12,512,512]{1,2,0:T(8,128)}) fusion(f32[12,512,512]{1,2,0:T(8,128)S(1)} %fusion.138, f32[12,512]{1,0:T(8,128)S(1)} %dynamic-slice_bitcast_fusion.2, pred[512,512]{0,1:T(8,128)(4,1)S(1)} %broadcast_compare_fusion.5, bf16[2,512,12,64]{1,3,2,0:T(8,128)(2,1)S(1)} %copy-done.10, ...), kind=kOutput, calls=%fused_computation.25.clone.1 | convolution fusion | flops 418375680 | bytes 27059200 | tf_op jit(solution)/shard_map/while/body/eval_jaxpr/qhd,khd->hqk/dot_general | solution.py:127
  307.9 7.1 %multiply_convert_fusion.5 = bf16[12,512,512]{1,2,0:T(8,128)(2,1)S(1)} fusion(f32[12,512,512]{1,2,0:T(8,128)} %get-tuple-element.405, f32[12,512,512]{1,2,0:T(8,128)S(1)} %fusion.138, f32[12,512]{1,0:T(8,128)S(1)} %get-tuple-element.406, f32[12,512]{1,0:T(8,128)S(1)} %dynamic-slice_bitcast_fusion.2, pred[512,512]{0,1:T(8,128)(4,1)S(1)} %broadcast_compare_fusion.5), kind=kLoop, calls=%fused_computation.24.clone.1 | loop fusion | flops 18874368 | bytes 31768576 | tf_op jit(solution)/shard_map/while/body/eval_jaxpr/convert_element_type | solution.py:131
  319.5 3.0 copy.100
  322.9 3.1 copy.101
  331.2 5.7 convolution_convert_fusion.2
  337.0 9.1 %convolution_convert_fusion = bf16[3072,768]{1,0:T(8,128)(2,1)} fusion(bf16[1024,3072]{1,0:T(8,128)(2,1)} %get-tuple-element.273, bf16[1024,768]{1,0:T(8,128)(2,1)} %param.22), kind=kOutput, calls=%fused_computation.83 | convolution fusion | flops 4834197504 | bytes 12582912 | tf_op jit(solution)/shard_map/ta,tb->ab/dot_general | solution.py:27
  346.8 10.0 %convolution_convert_fusion.1 = bf16[768,3072]{1,0:T(8,128)(2,1)} fusion(bf16[1024,3072]{1,0:T(8,128)(2,1)} %get-tuple-element.290, f32[1024,768]{0,1:T(8,128)} %copy-done.7, f32[768]{0:T(1024)S(1)} %copy-done.51, f32[768]{0:T(1024)S(1)} %copy-done.43, f32[1024]{0:T(1024)S(1)} %copy-done.45, f32[1024]{0:T(1024)S(1)} %copy-done.35), kind=kOutput, calls=%fused_computation.84 | convolution fusion | flops 4838129664 | bytes 14170112 | tf_op jit(solution)/shard_map/ta,tb->ab/dot_general | solution.py:27
  359.3 4.3 all-gather.9
  365.4 19.4 %reduce-scatter.5.cloned.1.call-done = bf16[384,2304]{1,0:T(8,128)(2,1)} async-done(((bf16[768,2304]{1,0:T(8,128)(2,1)}), bf16[384,2304]{1,0:T(8,128)(2,1)}) %reduce-scatter.5.cloned.1.call-update) | async-done | bytes 1769488 | tf_op jit(solution)/shard_map/reduce_scatter | solution.py:245
  384.8 62.3 %reduce-scatter.11.cloned.1.call-done = bf16[1536,768]{1,0:T(8,128)(2,1)} async-done(((bf16[3072,768]{1,0:T(8,128)(2,1)}), bf16[1536,768]{1,0:T(8,128)(2,1)}) %reduce-scatter.11.cloned.1.call-update) | async-done | bytes 2359312 | tf_op jit(solution)/shard_map/reduce_scatter | solution.py:199
  447.1 63.0 %reduce-scatter.9.cloned.1.call-done = bf16[384,3072]{1,0:T(8,128)(2,1)} async-done(((bf16[768,3072]{1,0:T(8,128)(2,1)}), bf16[384,3072]{1,0:T(8,128)(2,1)}) %reduce-scatter.9.cloned.1.call-update) | async-done | bytes 2359312 | tf_op jit(solution)/shard_map/reduce_scatter | solution.py:193
  510.2 10.0 %add_convert_fusion.3 = bf16[1024,768]{0,1:T(8,128)(2,1)} fusion(f32[1024,768]{0,1:T(8,128)} %copy-done.7, bf16[1024,3072]{1,0:T(8,128)(2,1)} %get-tuple-element.273, bf16[3072,768]{1,0:T(8,128)(2,1)} %all-gather.22.cloned.1.call-done, f32[768]{0:T(1024)S(1)} %reshape.254), kind=kOutput, calls=%fused_computation.106 | convolution fusion | flops 4834197504 | bytes 15731712 | tf_op jit(solution)/shard_map/dot_general | solution.py:23
  520.1 2.6 copy.105
  524.9 9.1 %fusion.87 = (bf16[768]{0:T(1024)(128)(2,1)S(1)}, f32[1024,768]{1,0:T(8,128)}) fusion(bf16[1024,2304]{0,1:T(8,128)(2,1)} %copy-done.25, bf16[768,2304]{1,0:T(8,128)(2,1)} %all-gather.16.cloned.1.call-done), kind=kOutput, calls=%fused_computation.140 | convolution fusion | flops 3624664320 | bytes 11404800 | tf_op jit(solution)/shard_map/tb,ab->ta/dot_general | solution.py:31
  534.0 3.6 copy.102
  537.6 2.6 fusion.73
  541.9 7.4 %all-reduce.11 = (bf16[768]{0:T(1024)(128)(2,1)S(1)}, bf16[768]{0:T(1024)(128)(2,1)S(1)}, bf16[768]{0:T(1024)(128)(2,1)S(1)}, bf16[768]{0:T(1024)(128)(2,1)S(1)}...) all-reduce(bf16[768]{0:T(1024)(128)(2,1)S(1)} %get-tuple-element.21, ...), channel_id=3, replica_groups=mesh['dp'=16,'fsdp'=2] {'fsdp'}, use_global_device_ids=true, to_apply=%region_16.17.clone | all-reduce | flops 9216 | bytes 36864
  550.0 61.8 %all-reduce.9 = (bf16[384]{0:T(512)(128)(2,1)S(1)}, bf16[384]{0:T(512)(128)(2,1)S(1)}, bf16[384]{0:T(512)(128)(2,1)S(1)}, bf16[384]{0:T(512)(128)(2,1)S(1)}, bf1...) all-reduce(bf16[384]{0:T(512)(128)(2,1)S(1)} %dynamic-slice.3, ...), channel_id=1, replica_groups=mesh['dp'=16,'fsdp'=2] {'dp'}, use_global_device_ids=true, to_apply=%region_20.21 | all-reduce | flops 4224 | bytes 16896 | tf_op jit(solution)/shard_map/psum | solution.py:265
  615.9 6.0 add_convert_fusion.2
  621.9 2.6 copy.106
  625.1 17.5 %all-gather.10 = bf16[16,1,384]{2,1,0:T(2,128)(2,1)S(1)} all-gather(bf16[1,1,384]{2,1,0:T(2,128)(2,1)S(1)} %reshape.244), channel_id=2, replica_groups=mesh['dp'=16,'fsdp'=2] {'dp'}, dimensions={0}, use_global_device_ids=true | all-gather | bytes 13056 | tf_op jit(solution)/shard_map/all_gather | solution.py:262
  643.2 23.0 %all-reduce.14.cloned.1.call-done = (bf16[384,2304]{1,0:T(8,128)(2,1)}, bf16[384,768]{1,0:T(8,128)(2,1)}, bf16[384,3072]{1,0:T(8,128)(2,1)}, bf16[1536,768]{1,0:T(8,128)(2,1)}) async-done(((bf16[384,2304]{1,0:T(8,128)(2,1)}, bf16[384,768]{1,0:T(8,128)(2,1)}, bf16[384,3072]{1,0:T(8,128)(2,1)}, bf16[1536,768]{1,0:T(8,128)(2,1)}), (bf16[384,2304]{1,0:T(8,128)(2,1)}, bf16[384,768]{1,0:T(8,128)(2,1)}, ...) | async-done | bytes 7077904 | tf_op jit(solution)/shard_map/psum | solution.py:266
  668.5 3.5 convert_element_type.270
  672.0 2.8 convert_element_type.281
  674.8 2.5 convert_element_type.284
  (285 shorter events, 67.6 us)
Async XLA Ops:
  7.2 3.6 copy-start.24
  7.2 56.1 %all-gather.16.cloned.1.call-start = ((), (), s32[]{:S(2)}) async-start(), calls=%async_computation.4 | async-start | bytes 5308416 | tf_op jit(solution)/shard_map/all_gather | solution.py:81
  10.7 112.6 %all-gather.18.cloned.1.call-start = ((), (), s32[]{:S(2)}) async-start(), calls=%async_computation.5 | async-start | bytes 1769472 | tf_op jit(solution)/shard_map/all_gather | solution.py:84
  11.7 141.4 %all-gather.20.cloned.1.call-start = ((), (), s32[]{:S(2)}) async-start(), calls=%async_computation.6 | async-start | bytes 7077888 | tf_op jit(solution)/shard_map/all_gather | solution.py:88
  15.8 4.2 copy-start.55
  15.9 4.2 copy-start.56
  15.9 4.3 copy-start.57
  15.9 4.3 copy-start.58
  15.9 4.3 copy-start.59
  15.9 4.3 copy-start.60
  15.9 4.3 copy-start.61
  15.9 36.0 %copy-start.54 = (s32[1024]{0:T(1024)S(1)}, s32[1024]{0:T(1024)}, u32[]{:S(2)}) copy-start(s32[1024]{0:T(1024)} %param.21) | copy-start | bytes 12292
  15.9 36.0 %copy-start.48 = (f32[1536]{0:T(1024)S(1)}, f32[1536]{0:T(1024)}, u32[]{:S(2)}) copy-start(f32[1536]{0:T(1024)} %param.33) | copy-start | bytes 18436
  16.0 201.8 %all-gather.22.cloned.1.call-start = ((), (), s32[]{:S(2)}) async-start(), calls=%async_computation.7 | async-start | bytes 7077888 | tf_op jit(solution)/shard_map/all_gather | solution.py:90
  20.0 345.4 %reduce-scatter.7.cloned.1.call-start = ((), (), s32[]{:S(2)}) async-start(), calls=%async_computation.9 | async-start | bytes 1769472 | tf_op jit(solution)/shard_map/reduce_scatter | solution.py:254
  25.6 127.4 %copy-start.50 = (f32[768]{0:T(1024)}, f32[768]{0:T(1024)S(1)}, u32[]{:S(2)}) copy-start(f32[768]{0:T(1024)S(1)} %reshape.252) | copy-start | bytes 9220
  30.0 224.0 %copy-start.42 = (f32[768]{0:T(1024)}, f32[768]{0:T(1024)S(1)}, u32[]{:S(2)}) copy-start(f32[768]{0:T(1024)S(1)} %reshape.251) | copy-start | bytes 9220
  47.5 15.8 %copy-start.52 = (f32[768]{0:T(1024)}, f32[768]{0:T(1024)S(1)}, u32[]{:S(2)}) copy-start(f32[768]{0:T(1024)S(1)} %reshape.247) | copy-start | bytes 9220
  51.9 11.4 %copy-start.32 = (f32[768]{0:T(1024)}, f32[768]{0:T(1024)S(1)}, u32[]{:S(2)}) copy-start(f32[768]{0:T(1024)S(1)} %reshape.246) | copy-start | bytes 9220
  56.4 2.6 copy-start.17
  58.3 11.4 %copy-start.4 = (bf16[1024,768]{0,1:T(8,128)(2,1)}, bf16[1024,768]{0,1:T(8,128)(2,1)S(1)}, u32[]{:S(2)}) copy-start(bf16[1024,768]{0,1:T(8,128)(2,1)S(1)} %copy.83) | copy-start | bytes 4718596
  58.6 11.1 %copy-start.30 = (f32[1024]{0:T(1024)}, f32[1024]{0:T(1024)S(1)}, u32[]{:S(2)}) copy-start(f32[1024]{0:T(1024)S(1)} %broadcast_multiply_fusion.1) | copy-start | bytes 12292
  59.0 10.7 %copy-start.40 = (f32[1024]{0:T(1024)}, f32[1024]{0:T(1024)S(1)}, u32[]{:S(2)}) copy-start(f32[1024]{0:T(1024)S(1)} %fusion.72) | copy-start | bytes 12292
  59.1 10.6 %copy-start.36 = (f32[1024]{0:T(1024)}, f32[1024]{0:T(1024)S(1)}, u32[]{:S(2)}) copy-start(f32[1024]{0:T(1024)S(1)} %fusion.76) | copy-start | bytes 12292
  73.3 5.8 copy-start.18
  117.5 5.8 copy-start
  117.5 5.8 copy-start.2
  117.5 5.8 copy-start.26
  117.5 5.8 copy-start.28
  127.1 126.9 %copy-start.7 = (f32[1024,768]{0,1:T(8,128)}, f32[1024,768]{0,1:T(8,128)S(1)}, u32[]{:S(2)}) copy-start(f32[1024,768]{0,1:T(8,128)S(1)} %get-tuple-element.283) | copy-start | bytes 9437188
  127.2 126.9 %copy-start.34 = (f32[1024]{0:T(1024)}, f32[1024]{0:T(1024)S(1)}, u32[]{:S(2)}) copy-start(f32[1024]{0:T(1024)S(1)} %broadcast_multiply_fusion) | copy-start | bytes 12292
  127.6 126.5 %copy-start.44 = (f32[1024]{0:T(1024)}, f32[1024]{0:T(1024)S(1)}, u32[]{:S(2)}) copy-start(f32[1024]{0:T(1024)S(1)} %fusion.77) | copy-start | bytes 12292
  250.5 3.5 copy-start.8
  255.4 2.0 copy-start.23
  259.9 124.9 %reduce-scatter.5.cloned.1.call-start = ((), (), s32[]{:S(2)}) async-start(), calls=%async_computation.8 | async-start | bytes 5308416 | tf_op jit(solution)/shard_map/reduce_scatter | solution.py:245
  266.5 4.0 copy-start.1
  266.5 4.0 copy-start.3
  266.5 4.0 copy-start.27
  266.5 4.0 copy-start.29
  270.8 1.9 copy-start.11
  272.7 4.0 copy-start.10
  283.5 7.1 %copy-start.19 = (bf16[2,512,12,64]{1,3,2,0:T(8,128)(2,1)S(1)}, bf16[2,512,12,64]{1,3,2,0:T(8,128)(2,1)}, u32[]{:S(2)}) copy-start(bf16[2,512,12,64]{1,3,2,0:T(8,128)(2,1)} %get-tuple-element.444) | copy-start | bytes 4718596 | tf_op jit(solution)/shard_map/while
  290.6 2.0 copy-start.14
  295.2 1.9 copy-start.11
  297.0 4.0 copy-start.10
  307.9 7.1 %copy-start.19 = (bf16[2,512,12,64]{1,3,2,0:T(8,128)(2,1)S(1)}, bf16[2,512,12,64]{1,3,2,0:T(8,128)(2,1)}, u32[]{:S(2)}) copy-start(bf16[2,512,12,64]{1,3,2,0:T(8,128)(2,1)} %get-tuple-element.444) | copy-start | bytes 4718596 | tf_op jit(solution)/shard_map/while
  315.0 2.0 copy-start.14
  322.9 3.6 copy-start.16
  328.7 2.5 copy-start.5
  328.7 2.5 copy-start.31
  328.7 2.5 copy-start.33
  328.7 2.5 copy-start.37
  328.7 2.5 copy-start.53
  329.0 2.2 copy-start.25
  336.9 110.2 %reduce-scatter.11.cloned.1.call-start = ((), (), s32[]{:S(2)}) async-start(), calls=%async_computation.11 | async-start | bytes 7077888 | tf_op jit(solution)/shard_map/reduce_scatter | solution.py:199
  346.2 164.0 %reduce-scatter.9.cloned.1.call-start = ((), (), s32[]{:S(2)}) async-start(), calls=%async_computation.10 | async-start | bytes 7077888 | tf_op jit(solution)/shard_map/reduce_scatter | solution.py:193
  356.8 2.5 copy-start.62
  356.8 309.4 %all-reduce.14.cloned.1.call-start = ((), (), s32[]{:S(2)}) async-start(), calls=%async_computation.12 | async-start | bytes 14155776 | tf_op jit(solution)/shard_map/psum | solution.py:266
  537.6 2.6 copy-start.41
  537.6 3.0 copy-start.6
  540.3 75.6 %copy-start.13 = (bf16[1024,768]{0,1:T(8,128)(2,1)S(1)}, bf16[1024,768]{0,1:T(8,128)(2,1)}, u32[]{:S(2)}) copy-start(bf16[1024,768]{0,1:T(8,128)(2,1)} %copy.92) | copy-start | bytes 4718596
  540.3 75.6 %copy-start.39 = (f32[1024]{0:T(1024)S(1)}, f32[1024]{0:T(1024)}, u32[]{:S(2)}) copy-start(f32[1024]{0:T(1024)} %copy-done.38) | copy-start | bytes 12292
  666.2 5.8 copy-start.22
  672.0 2.8 copy-start.21
  (16 other events, 19.4 us)
Sparse Core Ops, SparseCore 0:
  10.8 52.3 all-gather.15
  65.4 22.7 all-gather.17
  90.4 62.6 all-gather.19
  155.0 62.6 all-gather.21
  260.0 21.7 reduce-scatter.6
  337.0 47.6 reduce-scatter.4
  387.1 59.9 reduce-scatter.10
  450.1 59.9 reduce-scatter.8
  514.2 152.0 all-reduce.13
